TPU v7x, 1024 devices: a whole 4x8x16 slice. The times are simulated.
1024 devices in a mesh: seq: 16 (over z), exp: 16 (over y, core), head: 4 (over x).
Axes of the slice: x: 4, y: 8, z: 16, core: 2. Of those that a mesh axis runs over, the one named last changes fastest.
Arguments:
- query: bfloat16 [16, 8192, 2048], P('exp', 'seq', 'head'), may hold values from -6 to 6
- keys: bfloat16 [16, 8192, 2048], P('exp', 'seq', 'head'), may hold values from -6 to 6
- values: bfloat16 [16, 8192, 2048], P('exp', 'seq', 'head'), may hold values from -24 to 24
- attn_gain: float32 [2048], P('head'), may hold values from 0.5 to 1.5
- w_out: bfloat16 [2048, 2048], P('head'), may hold values from -0.125 to 0.125
- tokens: bfloat16 [16, 8192, 2048], P('exp', ('seq', 'head')), may hold values from -24 to 24
- routes: int32 [16, 8192, 2], P('exp', ('seq', 'head')), may hold values from 0 to 63, all different within a row; in each aligned block of 128 rows (0 to 127, 128 to 255, ..., all dimensions but the last counted through in order) at most 6 rows name the same one
- gates: float32 [16, 8192, 2], P('exp', ('seq', 'head')), may hold values from 0.25 to 1
- moe_gain: float32 [2048], replicated, may hold values from 0.5 to 1.5
- w_gate: bfloat16 [64, 2048, 384], P(('exp', 'head')), may hold values from -0.125 to 0.125
- w_up: bfloat16 [64, 2048, 384], P(('exp', 'head')), may hold values from -0.125 to 0.125
- w_down: bfloat16 [64, 384, 2048], P(('exp', 'head')), may hold values from -0.3125 to 0.3125
Outputs:
- mixed: bfloat16 [16, 8192, 2048], P('exp', ('seq', 'head'))
Inputs may be any that keep to these rules, and one draw needn't show every extreme that they name: `routes`: the 2 picks of a token are different experts. In each aligned block of 128 tokens (the rows of one device) no expert is picked more than 6 times, and some expert is picked exactly 6 times in some blocks.
All inputs are finite; a program needn't handle non-finite values.
Results may differ from a plain program's by a relative error of at most 0.0049.
Values may be sent and summed in bfloat16 or wider, within the bound.
No kernel may reach another device: no remote copies, remote signals or barrier semaphores. Data moves between devices by JAX's collectives and lax.ppermute only.
A program may use at most 64 MiB of HBM per device.

v0:
```python
import jax
import jax.numpy as jnp
from jax import lax
from jax.sharding import PartitionSpec as P

HEAD_DIM = 128
TOPK = 2
BLOCK = 512


EPSILON = 1e-06


def prefix_2(array, axis, combine, identity):
    peers, here = (lax.axis_size(axis), lax.axis_index(axis))
    everything = lax.all_gather(array, axis)
    start = jnp.broadcast_to(jnp.asarray(identity, array.dtype), array.shape)

    def lap(k, before):
        reached = k < here
        new = combine(before, everything[k])
        return jnp.where(reached, new, before)

    return lax.fori_loop(0, peers, lap, start)


def rms_scale(values_in, gain_vec):
    mean_square = jnp.mean(values_in * values_in, axis=-1, keepdims=True)
    return values_in * lax.rsqrt(mean_square + EPSILON) * gain_vec


def add_states(earlier, later):
    return earlier + later


def heads_first(array_in, n_blocks, head_count):
    shaped = array_in.reshape(n_blocks, BLOCK, head_count, HEAD_DIM)
    return shaped.transpose(0, 2, 1, 3)


def on_device(
    query, keys, values, attn_gain, w_out, tokens, routes, gates, moe_gain, w_gate, w_up, w_down
):
    seq_rows = query.shape[1]
    feat_width = query.shape[2]
    head_count = feat_width // HEAD_DIM
    n_blocks = seq_rows // BLOCK
    query_blk = heads_first(query[0], n_blocks, head_count)
    keys_blk = heads_first(keys[0], n_blocks, head_count)
    values_blk = heads_first(values[0], n_blocks, head_count)
    states = jnp.einsum("nhbd,nhbe->nhde", keys_blk, values_blk, preferred_element_type=jnp.float32)
    running = jnp.cumsum(states, axis=0)
    local_total = running[-1]
    carried = prefix_2(local_total, "seq", add_states, jnp.zeros_like(local_total))
    local_prefix = jnp.concatenate([jnp.zeros_like(states), running[:-1]], axis=0)
    prefix = (carried[None] + local_prefix).astype(jnp.bfloat16)
    causal = jnp.arange(BLOCK)[:, None] >= jnp.arange(BLOCK)[None, :]
    scores = jnp.einsum("nhtd,nhsd->nhts", query_blk, keys_blk, preferred_element_type=jnp.float32)
    scores = jnp.where(causal[None, None, :, :], scores, jnp.zeros_like(scores)).astype(
        jnp.bfloat16
    )
    inner_sum = jnp.einsum(
        "nhts,nhse->nhte", scores, values_blk, preferred_element_type=jnp.float32
    )
    outer_sum = jnp.einsum("nhtd,nhde->nhte", query_blk, prefix, preferred_element_type=jnp.float32)
    heads_out = inner_sum + outer_sum
    normed = rms_scale(heads_out, attn_gain.reshape(head_count, 1, HEAD_DIM)).astype(jnp.bfloat16)
    normed = normed.transpose(0, 2, 1, 3).reshape(seq_rows, feat_width)
    tok_rows = tokens.shape[1]
    model_width = tokens.shape[2]
    owned = lax.all_to_all(normed, "head", split_axis=0, concat_axis=1, tiled=True)
    attn_out = jnp.dot(
        owned, lax.all_gather(w_out, "head", axis=0, tiled=True), preferred_element_type=jnp.float32
    )
    resid = tokens[0].astype(jnp.float32) + attn_out
    moe_in = rms_scale(resid, moe_gain).astype(jnp.bfloat16)
    exp_local = w_gate.shape[0]
    n_exp = lax.axis_size("exp")
    n_head = lax.axis_size("head")
    expert_count = exp_local * n_exp * n_head
    capacity = max(2, tok_rows * TOPK * 3 // (expert_count * 2))
    slot_total = expert_count * capacity
    picks = routes[0].reshape(-1)
    matches = (picks[:, None] == jnp.arange(expert_count, dtype=jnp.int32)[None, :]).astype(
        jnp.int32
    )
    earlier = jnp.cumsum(matches, axis=0) - matches
    position = jnp.sum(earlier * matches, axis=1)
    slot_pairs = (picks * capacity + position).reshape(tok_rows, TOPK)
    slot_range = jnp.arange(slot_total, dtype=jnp.int32)[None, :]
    placed = jnp.zeros((tok_rows, slot_total), jnp.bfloat16)
    for pick in range(TOPK):
        placed = placed + (slot_pairs[:, pick : pick + 1] == slot_range).astype(jnp.bfloat16)
    buffer = jnp.einsum("ts,td->sd", placed, moe_in, preferred_element_type=jnp.float32).astype(
        jnp.bfloat16
    )
    buffer = buffer.reshape(expert_count, capacity, model_width)
    received = lax.all_to_all(buffer, ("exp", "head"), split_axis=0, concat_axis=0, tiled=True)
    sources = received.shape[0] // exp_local
    grouped = received.reshape(sources, exp_local, received.shape[1], received.shape[2])
    gate_part = jnp.einsum("secd,edf->secf", grouped, w_gate, preferred_element_type=jnp.float32)
    up_part = jnp.einsum("secd,edf->secf", grouped, w_up, preferred_element_type=jnp.float32)
    hidden = (jax.nn.silu(gate_part) * up_part).astype(jnp.bfloat16)
    expert_out = jnp.einsum("secf,efd->secd", hidden, w_down, preferred_element_type=jnp.float32)
    returned = lax.all_to_all(
        expert_out.astype(jnp.bfloat16).reshape(received.shape),
        ("exp", "head"),
        split_axis=0,
        concat_axis=0,
        tiled=True,
    )
    returned = returned.reshape(slot_total, model_width)
    gate_rows = gates[0]
    moe_sum = jnp.zeros((tok_rows, model_width), jnp.float32)
    for pick in range(TOPK):
        chosen = returned[slot_pairs[:, pick]].astype(jnp.float32)
        moe_sum = moe_sum + gate_rows[:, pick : pick + 1] * chosen
    mixed = (resid + moe_sum).astype(jnp.bfloat16)
    return mixed[None]


def solution(mesh):
    in_specs = (
        P("exp", "seq", "head"),
        P("exp", "seq", "head"),
        P("exp", "seq", "head"),
        P("head"),
        P("head", None),
        P("exp", ("seq", "head"), None),
        P("exp", ("seq", "head"), None),
        P("exp", ("seq", "head"), None),
        P(),
        P(("exp", "head"), None, None),
        P(("exp", "head"), None, None),
        P(("exp", "head"), None, None),
    )
    out_specs = P("exp", ("seq", "head"), None)
    return jax.shard_map(
        on_device, mesh=mesh, in_specs=in_specs, out_specs=out_specs, check_vma=False
    )
```

profile of v0, /device:TPU:2, one launch (start us, length us, event | category | flops | bytes accessed | tf_op | source)
XLA Modules:
  0.0 346.8 jit_solution(16956354578041208478)
XLA Ops:
  6.5 1.3 fusion.55
  7.8 1.1 fusion.56
  9.1 1.1 fusion.58
  10.2 0.7 all-gather.4.cloned.1.call-update
  11.3 0.6 fusion.52
  11.9 1.3 reduce-window.6
  13.5 0.8 iota_compare_fusion
  14.5 85.1 %all-gather.6.cloned.1.call-done = f32[64,128,128]{2,1,0:T(8,128)} async-done(((f32[4,128,128]{2,1,0:T(8,128)}), f32[64,128,128]{2,1,0:T(8,128)}) %all-gather.6.cloned.1.call-update) | async-done | bytes 4194320 | tf_op jit(solution)/shard_map/all_gather | solution.py:16
  99.6 17.0 %while.14 = (s32[]{:T(128)}, f32[4,128,128]{2,1,0:T(8,128)S(1)}, s32[]{:T(128)}, f32[16,4,128,128]{3,2,1,0:T(8,128)}, s32[]{:T(128)}, /*index=5*/s32[]{:T(128)}) while((s32[]{:T(128)}, f32[4,128,128]{2,1,0:T(8,128)S(1)}, s32[]{:T(128)}, f32[16,4,128,128]{3,2,1,0:T(8,128)}, s32[]{:T(128)}, /*index=5*/s32[]{:T(128)}) %tuple.55), condition=%wide.region_1.2_spmd.clone, body=%wide.region_0.0_spmd.clone.sunk | while | flops 196612 | bytes 786525 | solution.py:24
  99.6 1.0 add_select_fusion.2
  100.6 1.0 add_select_fusion.2
  101.7 1.0 add_select_fusion.2
  102.8 1.0 add_select_fusion.2
  103.8 1.0 add_select_fusion.2
  104.9 1.0 add_select_fusion.2
  105.9 1.0 add_select_fusion.2
  107.0 1.0 add_select_fusion.2
  108.1 1.0 add_select_fusion.2
  109.1 1.0 add_select_fusion.2
  110.2 1.0 add_select_fusion.2
  111.3 1.0 add_select_fusion.2
  112.3 1.0 add_select_fusion.2
  113.4 1.0 add_select_fusion.2
  114.5 1.0 add_select_fusion.2
  115.5 1.0 add_select_fusion.2
  116.6 1.4 fusion.40
  118.0 3.9 %multiply_reduce_fusion.1 = (f32[4,512]{1,0:T(4,128)S(1)}, f32[4,512,128]{1,2,0:T(8,128)}) fusion(f32[4,512,128]{1,2,0:T(8,128)} %fusion.40, bf16[4,512,128]{2,1,0:T(8,128)(2,1)S(1)} %bitcast.111, bf16[4,512,128]{2,1,0:T(8,128)(2,1)S(1)} %bitcast.109, bf16[4,512,128]{2,1,0:T(8,128)(2,1)S(1)} %bitcast.113, pred[512,512]{1,0:T(8,128)(4,1)} %iota_compare_fusion), kind=kOutput, calls=%fused_computation.25 | convolution fusion | flops 539752448 | bytes 3940352 | tf_op jit(solution)/shard_map/nhts,nhse->nhte/dot_general | solution.py:62
  121.9 1.5 fusion.33
  123.5 0.9 copy.39
  124.4 4.8 %all-to-all-start = ((bf16[4,128,512]{1,2,0:T(8,128)(2,1)}), bf16[4,128,512]{1,2,0:T(8,128)(2,1)S(1)}, u32[]{:S(2)}, u32[]{:S(2)}) async-start(bf16[4,128,512]{1,2,0:T(8,128)(2,1)} %copy.39), calls=%async_computation | async-start | bytes 1048576 | tf_op jit(solution)/shard_map/all_to_all | solution.py:71
  129.5 0.2 fusion.47
  129.7 11.9 %all-to-all-done = bf16[4,128,512]{1,2,0:T(8,128)(2,1)S(1)} async-done(((bf16[4,128,512]{1,2,0:T(8,128)(2,1)}), bf16[4,128,512]{1,2,0:T(8,128)(2,1)S(1)}, u32[]{:S(2)}, u32[]{:S(2)}) %all-to-all-start) | async-done | bytes 524320 | tf_op jit(solution)/shard_map/all_to_all | solution.py:71
  141.6 54.5 %all-gather.4.cloned.1.call-done = bf16[2048,2048]{1,0:T(8,128)(2,1)} async-done(((bf16[512,2048]{1,0:T(8,128)(2,1)}), bf16[2048,2048]{1,0:T(8,128)(2,1)}) %all-gather.4.cloned.1.call-update) | async-done | bytes 8388624 | tf_op jit(solution)/shard_map/all_gather | solution.py:73
  196.0 4.8 %multiply_reduce_fusion = (f32[128]{0:T(128)S(1)}, f32[128,2048]{1,0:T(8,128)S(1)}) fusion(bf16[128,2048]{0,1:T(8,128)(2,1)S(1)} %bitcast.107, bf16[2048,2048]{1,0:T(8,128)(2,1)} %all-gather.4.cloned.1.call-done, bf16[1,128,2048]{2,1,0:T(8,128)(2,1)S(1)} %copy-done.3), kind=kOutput, calls=%fused_computation.23 | convolution fusion | flops 1074790272 | bytes 10486272 | tf_op jit(solution)/shard_map/dot_general | solution.py:72
  200.8 1.0 copy-done.1
  201.8 0.7 convolution_convert_fusion.1
  202.5 1.6 reshape.129
  204.1 60.7 %all_to_all.29 = bf16[64,6,2048]{2,1,0:T(8,128)(2,1)S(1)} all-to-all(bf16[64,6,2048]{2,1,0:T(8,128)(2,1)} %reshape.129), channel_id=1, replica_groups=mesh['seq'=16,'exp'=16,'head'=4] {'exp','head'}, dimensions={0} | all-to-all | bytes 3145728 | tf_op jit(solution)/shard_map/all_to_all | solution.py:98
  264.8 1.3 copy-done.2
  266.1 1.9 fusion.7
  268.0 4.1 %convolution_convert_fusion = bf16[64,6,2048]{2,0,1:T(8,128)(2,1)S(1)} fusion(bf16[1,384,2048]{2,1,0:T(8,128)(2,1)S(1)} %copy-done, bf16[1,2048,384]{2,1,0:T(8,128)(2,1)} %param.24, bf16[64,6,2048]{2,1,0:T(8,128)(2,1)} %copy-done.2, f32[64,1,6,384]{3,0,2,1:T(8,128)} %fusion.7), kind=kOutput, calls=%fused_computation.4 | convolution fusion | flops 1209630720 | bytes 6881280 | tf_op jit(solution)/shard_map/secf,efd->secd/dot_general | solution.py:104
  272.2 2.2 copy.46
  274.4 5.7 %all-to-all-start.2 = ((bf16[64,6,2048]{2,1,0:T(8,128)(2,1)}), bf16[64,6,2048]{2,1,0:T(8,128)(2,1)}, u32[]{:S(2)}, u32[]{:S(2)}) async-start(bf16[64,6,2048]{2,1,0:T(8,128)(2,1)} %copy.46), calls=%async_computation.2 | async-start | bytes 4194304 | tf_op jit(solution)/shard_map/all_to_all | solution.py:105
  280.2 51.1 %all-to-all-done.2 = bf16[64,6,2048]{2,1,0:T(8,128)(2,1)} async-done(((bf16[64,6,2048]{2,1,0:T(8,128)(2,1)}), bf16[64,6,2048]{2,1,0:T(8,128)(2,1)}, u32[]{:S(2)}, u32[]{:S(2)}) %all-to-all-start.2) | async-done | bytes 1572896 | tf_op jit(solution)/shard_map/all_to_all | solution.py:105
  331.3 2.6 reshape.134
  333.9 1.7 gather_fusion
  335.6 1.7 gather_fusion.1
  337.4 2.6 fusion.34
  (43 shorter events, 1.3 us)
Async XLA Ops:
  6.5 261.5 %copy-start = (bf16[1,384,2048]{2,1,0:T(8,128)(2,1)S(1)}, bf16[1,384,2048]{2,1,0:T(8,128)(2,1)}, u32[]{:S(2)}) copy-start(bf16[1,384,2048]{2,1,0:T(8,128)(2,1)} %param.25) | copy-start | bytes 4718596
  6.5 93.0 %all-gather.6.cloned.1.call-start = ((), (), s32[]{:S(2)}) async-start(), calls=%async_computation.4 | async-start | bytes 4456448 | tf_op jit(solution)/shard_map/all_gather | solution.py:16
  9.0 1.9 copy-start.8
  10.1 4.2 %copy-start.4 = (bf16[1,512,512]{2,1,0:T(8,128)(2,1)S(1)}, bf16[1,512,512]{2,1,0:T(8,128)(2,1)}, u32[]{:S(2)}) copy-start(bf16[1,512,512]{2,1,0:T(8,128)(2,1)} %param.14) | copy-start | bytes 1572868
  10.1 185.9 %all-gather.4.cloned.1.call-start = ((), (), s32[]{:S(2)}) async-start(), calls=%async_computation.3 | async-start | bytes 10485760 | tf_op jit(solution)/shard_map/all_gather | solution.py:73
  13.5 86.1 %copy-start.6 = (s32[64,3]{0,1:T(4,128)}, s32[64,3]{0,1:T(4,128)S(1)}, u32[]{:S(2)}) copy-start(s32[64,3]{0,1:T(4,128)S(1)} %reduce-window.9) | copy-start | bytes 2308
  118.0 3.9 %copy-start.7 = (f32[512]{0:T(512)S(1)}, f32[512]{0:T(512)}, u32[]{:S(2)}) copy-start(f32[512]{0:T(512)} %param.17) | copy-start | bytes 6148
  123.4 5.8 %slice-start = ((s32[64,3]{0,1:T(4,128)}), s32[64,2]{0,1:T(2,128)S(1)}, s32[]{:S(2)}) async-start(s32[64,3]{0,1:T(4,128)} %copy-done.6), calls=%async_computation.5 | async-start | bytes 2048 | tf_op jit(solution)/shard_map/slice.1
  123.4 72.6 %copy-start.3 = (bf16[1,128,2048]{2,1,0:T(8,128)(2,1)S(1)}, bf16[1,128,2048]{2,1,0:T(8,128)(2,1)}, u32[]{:S(2)}) copy-start(bf16[1,128,2048]{2,1,0:T(8,128)(2,1)} %param.19) | copy-start | bytes 1572868
  124.4 17.2 %all-to-all-start = ((bf16[4,128,512]{1,2,0:T(8,128)(2,1)}), bf16[4,128,512]{1,2,0:T(8,128)(2,1)S(1)}, u32[]{:S(2)}, u32[]{:S(2)}) async-start(bf16[4,128,512]{1,2,0:T(8,128)(2,1)} %copy.39), calls=%async_computation | async-start | bytes 1048576 | tf_op jit(solution)/shard_map/all_to_all | solution.py:71
  196.0 5.7 %copy-start.5 = (f32[2048]{0:T(1024)S(1)}, f32[2048]{0:T(1024)}, u32[]{:S(2)}) copy-start(f32[2048]{0:T(1024)} %param.22) | copy-start | bytes 24580
  200.8 1.0 copy-start.1
  204.1 62.1 %copy-start.10 = (bf16[1,2048,384]{2,1,0:T(8,128)(2,1)S(1)}, bf16[1,2048,384]{2,1,0:T(8,128)(2,1)}, u32[]{:S(2)}) copy-start(bf16[1,2048,384]{2,1,0:T(8,128)(2,1)} %param.23) | copy-start | bytes 4718596
  264.8 1.3 copy-start.2
  274.4 5.8 %copy-start.9 = (f32[1,128,2]{1,2,0:T(2,128)S(1)}, f32[1,128,2]{1,2,0:T(2,128)}, u32[]{:S(2)}) copy-start(f32[1,128,2]{1,2,0:T(2,128)} %param.21) | copy-start | bytes 3076
  274.4 56.9 %all-to-all-start.2 = ((bf16[64,6,2048]{2,1,0:T(8,128)(2,1)}), bf16[64,6,2048]{2,1,0:T(8,128)(2,1)}, u32[]{:S(2)}, u32[]{:S(2)}) async-start(bf16[64,6,2048]{2,1,0:T(8,128)(2,1)} %copy.46), calls=%async_computation.2 | async-start | bytes 4194304 | tf_op jit(solution)/shard_map/all_to_all | solution.py:105
Sparse Core Ops, SparseCore 0:
  10.3 89.2 all-gather.5
  102.2 93.7 all-gather.3
where the time goes:
time: 348 us; the launch traced here: 347 us
  waiting for transfers between devices  203 us (58%)
  blocking collectives  60.7 us (17%)
  other arithmetic  24 us (7%)
  matrix products  17.8 us (5%)
  local copies, waits for them, and re-layouts  16.4 us (5%)
  between operations  13.6 us (4%)
  starting transfers between devices  10.6 us (3%)
    all_gather x1, waiting for transfers between devices, prefix_2(): everything = lax.all_gather(array, axis)  85.1 us
    all_to_all x1, blocking collectives, on_device(): lax.all_to_all(buffer, ('exp', 'head'), split_axis=0, concat_axis=0, tile...  60.7 us
    all_gather x1, waiting for transfers between devices, on_device(): lax.all_gather(w_out, 'head', axis=0, tiled=True)  54.5 us
    all_to_all x1, waiting for transfers between devices, on_device(): lax.all_to_all(expert_out.astype(jnp.bfloat16).reshape(received.shape), (...  51.1 us
    select_n x16, other arithmetic, lap(): return jnp.where(reached, new, before)  16.6 us
    all_to_all x1, waiting for transfers between devices, on_device(): lax.all_to_all(normed, 'head', split_axis=0, concat_axis=1, tiled=True)  11.9 us
  transfers between devices with their start and end apart: 4, of which 4 were waited for; matrix products, arithmetic and copies ran while one was open for 8% of the time, Pallas kernels for 0%

commit v1 on v0

v1 whole, which is shorter than its diff:
```python
import functools

import jax
import jax.numpy as jnp
from jax import lax
from jax.experimental import pallas as pl
from jax.experimental.pallas import tpu as pltpu
from jax.sharding import PartitionSpec as P

HEAD_DIM = 128
TOPK = 2
CAP = 6
QUARTERS = 4
GROUP = 8
EPSILON = 1e-06

BF16 = jnp.bfloat16
F32 = jnp.float32
I32 = jnp.int32


def vmem():
    return pl.BlockSpec(memory_space=pltpu.VMEM)


def dot(a, b, dims=((1,), (0,))):
    return lax.dot_general(a, b, (dims, ((), ())), preferred_element_type=F32)


def states_kernel(keys_ref, values_ref, out_ref):
    heads = keys_ref.shape[1] // HEAD_DIM
    for h in range(heads):
        cols = slice(h * HEAD_DIM, (h + 1) * HEAD_DIM)
        state = dot(keys_ref[:, cols], values_ref[:, cols], ((0,), (0,)))
        out_ref[cols, :] = state.astype(out_ref.dtype)


def scan_kernel(in_ref, out_ref):
    blocks = in_ref.shape[0]
    total = jnp.zeros(in_ref.shape[1:], F32)
    for b in range(blocks):
        out_ref[b] = total.astype(out_ref.dtype)
        total = total + in_ref[b].astype(F32)


def slots_kernel(routes_ref, cols_ref, rows_ref, *, experts):
    rows = routes_ref.shape[0]
    first, second = routes_ref[:, 0:1], routes_ref[:, 1:2]
    ids = lax.broadcasted_iota(I32, (rows, experts), 1)
    hit0 = (first == ids).astype(F32)
    hit1 = (second == ids).astype(F32)
    above = lax.broadcasted_iota(I32, (rows, rows), 0) > lax.broadcasted_iota(I32, (rows, rows), 1)
    before = dot(above.astype(F32).astype(BF16), (hit0 + hit1).astype(BF16))
    pos0 = jnp.sum(before * hit0, axis=1, keepdims=True)
    pos1 = jnp.sum(before * hit1, axis=1, keepdims=True)
    slot0 = first.astype(F32) * CAP + pos0
    slot1 = second.astype(F32) * CAP + pos1
    lane = lax.broadcasted_iota(I32, (rows, 128), 1)
    both = jnp.where(lane == 0, slot0, jnp.where(lane == 1, slot1, 0.0))
    cols_ref[...] = both.astype(I32)
    rows_ref[...] = both.T[0:8, :].astype(I32)


def attention_kernel(query_ref, keys_ref, values_ref, prefix_ref, gain_ref, w_ref, out_ref):
    i = pl.program_id(0)
    rows = query_ref.shape[0]
    length = keys_ref.shape[0]
    heads = query_ref.shape[1] // HEAD_DIM
    row_ids = lax.broadcasted_iota(I32, (rows, length), 0) + i * rows
    causal = row_ids >= lax.broadcasted_iota(I32, (rows, length), 1)
    parts = []
    for h in range(heads):
        cols = slice(h * HEAD_DIM, (h + 1) * HEAD_DIM)
        q = query_ref[:, cols]
        scores = dot(q, keys_ref[:, cols], ((1,), (1,)))
        scores = jnp.where(causal, scores, 0.0).astype(BF16)
        out = dot(scores, values_ref[:, cols]) + dot(q, prefix_ref[cols, :])
        scale = lax.rsqrt(jnp.mean(out * out, axis=-1, keepdims=True) + EPSILON)
        parts.append((out * scale * gain_ref[:, cols]).astype(BF16))
    normed = jnp.concatenate(parts, axis=1)
    out_ref[...] = dot(normed, w_ref[...]).astype(out_ref.dtype)


def row_keys(count, base):
    piece = QUARTERS * CAP
    r = lax.broadcasted_iota(I32, (count, 1), 0).astype(F32) + base
    e = jnp.floor((r + 0.5) * (1.0 / piece))
    rem = r - e * piece
    q = jnp.floor((rem + 0.5) * (1.0 / CAP))
    c = rem - q * CAP
    return (QUARTERS * (e * CAP + c) + q).astype(I32)


def dispatch_kernel(recv_ref, tokens_ref, gain_ref, rows_ref, resid_ref, out_ref):
    peers = recv_ref.shape[0]
    tok_rows, width = tokens_ref.shape
    attn = recv_ref[0].astype(F32)
    for p in range(1, peers):
        attn = attn + recv_ref[p].astype(F32)
    resid = tokens_ref[...].astype(F32) + attn
    resid_ref[...] = resid
    scale = lax.rsqrt(jnp.mean(resid * resid, axis=-1, keepdims=True) + EPSILON)
    moe_in = (resid * scale * gain_ref[...]).astype(BF16)
    part = width // QUARTERS
    stacked = jnp.concatenate([moe_in[:, q * part : (q + 1) * part] for q in range(QUARTERS)], axis=0)
    slots = rows_ref[...]
    key0 = jnp.concatenate([slots[0:1] * QUARTERS + q for q in range(QUARTERS)], axis=1)
    key1 = jnp.concatenate([slots[1:2] * QUARTERS + q for q in range(QUARTERS)], axis=1)
    total = out_ref.shape[0]
    chunk = total // 4
    for b in range(4):
        keys = row_keys(chunk, b * chunk)
        pick = ((keys == key0) | (keys == key1)).astype(F32).astype(BF16)
        out_ref[b * chunk : (b + 1) * chunk, :] = dot(pick, stacked).astype(BF16)


def regroup_matrix(to_pieces):
    n = GROUP * QUARTERS * CAP
    i = lax.broadcasted_iota(I32, (n, 1), 0).astype(F32)
    q = jnp.floor((i + 0.5) * (1.0 / (GROUP * CAP)))
    rem = i - q * (GROUP * CAP)
    p = jnp.floor((rem + 0.5) * (1.0 / CAP))
    c = rem - p * CAP
    source = (p * (QUARTERS * CAP) + q * CAP + c).astype(I32)
    j = lax.broadcasted_iota(I32, (n, n), 1)
    matrix = (source == j).astype(F32)
    if to_pieces:
        matrix = matrix.T
    return matrix.astype(BF16)


def expert_kernel(recv_ref, gate_ref, up_ref, down_ref, out_ref, x_ref):
    rows, part = recv_ref.shape
    n = GROUP * QUARTERS * CAP
    m = n // QUARTERS
    gather = regroup_matrix(False)
    for g in range(rows // n):
        block = dot(gather, recv_ref[g * n : (g + 1) * n, :]).astype(BF16)
        for q in range(QUARTERS):
            x_ref[g * m : (g + 1) * m, q * part : (q + 1) * part] = block[q * m : (q + 1) * m, :]
    x = x_ref[...]
    gate = dot(x, gate_ref[...])
    up = dot(x, up_ref[...])
    hidden = (gate / (1.0 + jnp.exp(-gate)) * up).astype(BF16)
    scatter = regroup_matrix(True)
    for g in range(rows // n):
        made = dot(hidden[g * m : (g + 1) * m, :], down_ref[...]).astype(BF16)
        block = jnp.concatenate([made[:, q * part : (q + 1) * part] for q in range(QUARTERS)], axis=0)
        out_ref[g * n : (g + 1) * n, :] = dot(scatter, block).astype(BF16)


def combine_kernel(back_ref, resid_ref, cols_ref, gates_ref, out_ref, y_ref):
    rows, part = back_ref.shape
    tok_rows = resid_ref.shape[0]
    n = GROUP * QUARTERS * CAP
    m = n // QUARTERS
    gather = regroup_matrix(False)
    for g in range(rows // n):
        block = dot(gather, back_ref[g * n : (g + 1) * n, :]).astype(BF16)
        for q in range(QUARTERS):
            y_ref[g * m : (g + 1) * m, q * part : (q + 1) * part] = block[q * m : (q + 1) * m, :]
    y = y_ref[...]
    slot_total = y.shape[0]
    ids = lax.broadcasted_iota(I32, (tok_rows, slot_total), 1)
    total = resid_ref[...]
    moe = jnp.zeros_like(total)
    for pick in range(TOPK):
        chosen = (cols_ref[:, pick : pick + 1] == ids).astype(F32).astype(BF16)
        moe = moe + gates_ref[:, pick : pick + 1] * dot(chosen, y)
    out_ref[...] = (total + moe).astype(out_ref.dtype)


def on_device(
    query, keys, values, attn_gain, w_out, tokens, routes, gates, moe_gain, w_gate, w_up, w_down
):
    query, keys, values = query[0], keys[0], values[0]
    tokens, routes, gates = tokens[0], routes[0], gates[0]
    w_gate, w_up, w_down = w_gate[0], w_up[0], w_down[0]
    length, feat = query.shape
    tok_rows, width = tokens.shape
    n_seq, n_exp, n_head = (lax.axis_size(a) for a in ("seq", "exp", "head"))
    experts = n_exp * n_head
    part = width // QUARTERS
    piece = QUARTERS * CAP

    states = pl.pallas_call(
        states_kernel,
        out_shape=jax.ShapeDtypeStruct((feat, HEAD_DIM), BF16),
        in_specs=[vmem(), vmem()],
        out_specs=vmem(),
        name="states",
    )(keys, values)
    spread = lax.all_to_all(states, "seq", split_axis=0, concat_axis=0, tiled=True)
    scanned = pl.pallas_call(
        scan_kernel,
        out_shape=jax.ShapeDtypeStruct((n_seq, feat // n_seq, HEAD_DIM), BF16),
        in_specs=[vmem()],
        out_specs=vmem(),
        name="scan",
    )(spread.reshape(n_seq, feat // n_seq, HEAD_DIM))
    prefix = lax.all_to_all(
        scanned.reshape(feat, HEAD_DIM), "seq", split_axis=0, concat_axis=0, tiled=True
    )

    slot_cols, slot_rows = pl.pallas_call(
        functools.partial(slots_kernel, experts=experts),
        out_shape=(
            jax.ShapeDtypeStruct((tok_rows, 128), I32),
            jax.ShapeDtypeStruct((8, tok_rows), I32),
        ),
        in_specs=[vmem()],
        out_specs=(vmem(), vmem()),
        name="slots",
    )(routes)

    partial_out = pl.pallas_call(
        attention_kernel,
        out_shape=jax.ShapeDtypeStruct((length, width), BF16),
        grid=(n_head,),
        in_specs=[
            pl.BlockSpec((length // n_head, feat), lambda i: (i, 0)),
            pl.BlockSpec((length, feat), lambda i: (0, 0)),
            pl.BlockSpec((length, feat), lambda i: (0, 0)),
            pl.BlockSpec((feat, HEAD_DIM), lambda i: (0, 0)),
            pl.BlockSpec((1, feat), lambda i: (0, 0)),
            pl.BlockSpec((feat, width), lambda i: (0, 0)),
        ],
        out_specs=pl.BlockSpec((length // n_head, width), lambda i: (i, 0)),
        name="attention",
    )(query, keys, values, prefix, attn_gain.reshape(1, feat), w_out)
    summed = lax.all_to_all(partial_out, "head", split_axis=0, concat_axis=0, tiled=True)

    resid, sent = pl.pallas_call(
        dispatch_kernel,
        out_shape=(
            jax.ShapeDtypeStruct((tok_rows, width), F32),
            jax.ShapeDtypeStruct((experts * piece, part), BF16),
        ),
        in_specs=[vmem()] * 4,
        out_specs=(vmem(), vmem()),
        name="dispatch",
    )(summed.reshape(n_head, tok_rows, width), tokens, moe_gain.reshape(1, width), slot_rows)
    received = lax.all_to_all(sent, ("exp", "head"), split_axis=0, concat_axis=0, tiled=True)
    made = pl.pallas_call(
        expert_kernel,
        out_shape=jax.ShapeDtypeStruct((experts * piece, part), BF16),
        in_specs=[vmem()] * 4,
        out_specs=vmem(),
        scratch_shapes=[pltpu.VMEM((experts * CAP, width), BF16)],
        name="experts",
    )(received, w_gate, w_up, w_down)
    returned = lax.all_to_all(made, ("exp", "head"), split_axis=0, concat_axis=0, tiled=True)
    mixed = pl.pallas_call(
        combine_kernel,
        out_shape=jax.ShapeDtypeStruct((tok_rows, width), BF16),
        in_specs=[vmem()] * 4,
        out_specs=vmem(),
        scratch_shapes=[pltpu.VMEM((experts * CAP, width), BF16)],
        name="combine",
    )(returned, resid, slot_cols, gates)
    return mixed[None]


def solution(mesh):
    in_specs = (
        P("exp", "seq", "head"),
        P("exp", "seq", "head"),
        P("exp", "seq", "head"),
        P("head"),
        P("head", None),
        P("exp", ("seq", "head"), None),
        P("exp", ("seq", "head"), None),
        P("exp", ("seq", "head"), None),
        P(),
        P(("exp", "head"), None, None),
        P(("exp", "head"), None, None),
        P(("exp", "head"), None, None),
    )
    out_specs = P("exp", ("seq", "head"), None)
    return jax.shard_map(
        on_device, mesh=mesh, in_specs=in_specs, out_specs=out_specs, check_vma=False
    )
```

time: 348 us -> 207 us (0.59)
  waiting for transfers between devices: 203 us -> 58.3 us
  blocking collectives: 60.7 us -> 102 us
  Pallas kernels: 0 us -> 31.4 us
  other arithmetic: 24 us -> 0 us
  matrix products: 17.8 us -> 0 us
  between operations: 13.6 us -> 0.03 us
  local copies, waits for them, and re-layouts: 16.4 us -> 3.96 us
    all_gather x2 -> x0, waiting for transfers between devices: 140 us -> none  [the longest x1 85.1 us: prefix_2(): everything = lax.all_gather(array, axis)]
    all_to_all x1 -> x3, blocking collectives: 60.7 us -> 102 us  [the longest x1 49.8 us: on_device(): lax.all_to_all(sent, ('exp', 'head'), split_axis=0, concat_axis=0, tiled=...]
    pallas_call x0 -> x7, Pallas kernels: none -> 31.4 us  [the longest x1 9.5 us: on_device(): pl.pallas_call(expert_kernel, out_shape=jax.ShapeDtypeStruct((experts * p...]
    dot_general x7 -> x0, matrix products: 17.8 us -> none  [the longest x1 4.75 us: on_device(): jnp.dot(owned, lax.all_gather(w_out, 'head', axis=0, tiled=True), preferr...]
    select_n x17 -> x0, other arithmetic: 16.9 us -> none  [the longest x16 16.6 us: lap(): return jnp.where(reached, new, before)]
    all_to_all x2, waiting for transfers between devices: 63 us -> 58.3 us  [the longest x1 39.3 us: on_device(): lax.all_to_all(made, ('exp', 'head'), split_axis=0, concat_axis=0, tiled=...]
    reshape x2 -> x0, local copies, waits for them, and re-layouts: 4.22 us -> none  [the longest x1 2.6 us: on_device(): returned = returned.reshape(slot_total, model_width)]
  transfers between devices with their start and end apart: 4 -> 2, of which waited for: 4 -> 2; matrix products, arithmetic and copies ran while one was open for 8% -> 1% of each run, Pallas kernels for 0% -> 1%
where the time goes in v1:
time: 207 us; the launch traced here: 206 us
  blocking collectives  102 us (49%)
  waiting for transfers between devices  58.3 us (28%)
  Pallas kernels  31.4 us (15%)
  starting transfers between devices  10.5 us (5%)
  local copies, waits for them, and re-layouts  3.96 us (2%)
    all_to_all x1, blocking collectives, on_device(): lax.all_to_all(sent, ('exp', 'head'), split_axis=0, concat_axis=0, tiled=...  49.8 us
    all_to_all x1, waiting for transfers between devices, on_device(): lax.all_to_all(made, ('exp', 'head'), split_axis=0, concat_axis=0, tiled=...  39.3 us
    all_to_all x1, blocking collectives, on_device(): lax.all_to_all(states, 'seq', split_axis=0, concat_axis=0, tiled=True)  33.8 us
    all_to_all x1, waiting for transfers between devices, on_device(): lax.all_to_all(partial_out, 'head', split_axis=0, concat_axis=0, tiled=True)  19 us
    all_to_all x1, blocking collectives, on_device(): lax.all_to_all(scanned.reshape(feat, HEAD_DIM), 'seq', split_axis=0, conc...  18.2 us
    pallas_call x1, Pallas kernels, on_device(): pl.pallas_call(expert_kernel, out_shape=jax.ShapeDtypeStruct((experts * p...  9.5 us
    pallas_call x1, Pallas kernels, on_device(): pl.pallas_call(attention_kernel, out_shape=jax.ShapeDtypeStruct((length,...  7.96 us
    all_to_all x1, starting transfers between devices, on_device(): lax.all_to_all(made, ('exp', 'head'), split_axis=0, concat_axis=0, tiled=...  5.56 us
  transfers between devices with their start and end apart: 2, of which 2 were waited for; matrix products, arithmetic and copies ran while one was open for 1% of the time, Pallas kernels for 1%

profile of v1, /device:TPU:2, one launch (start us, length us, event | category | flops | bytes accessed | tf_op | source)
XLA Modules:
  0.0 206.0 jit_solution(8224865440234697476)
XLA Ops:
  0.0 2.2 %states.1 = bf16[512,128]{1,0:T(8,128)(2,1)} custom-call(bf16[512,512]{1,0:T(8,128)(2,1)} %bitcast.23, bf16[512,512]{1,0:T(8,128)(2,1)} %bitcast.25), custom_call_target="tpu_custom_call" | custom-call | tf_op jit(solution)/shard_map/states/pallas_call | solution.py:186
  2.2 33.8 %all_to_all.48.in_ref = bf16[16,32,128]{2,1,0:T(8,128)(2,1)} all-to-all(bf16[16,32,128]{2,1,0:T(8,128)(2,1)} %bitcast.33), channel_id=1, replica_groups=mesh['seq'=16,'exp'=16,'head'=4] {'seq'}, dimensions={0} | all-to-all | bytes 262144 | tf_op jit(solution)/shard_map/all_to_all | solution.py:193
  36.0 1.6 scan.1
  37.5 18.2 %all_to_all.49 = bf16[16,32,128]{2,1,0:T(8,128)(2,1)} all-to-all(bf16[16,32,128]{2,1,0:T(8,128)(2,1)} %scan.1), channel_id=1, replica_groups=mesh['seq'=16,'exp'=16,'head'=4] {'seq'}, dimensions={0} | all-to-all | bytes 262144 | tf_op jit(solution)/shard_map/all_to_all | solution.py:201
  55.7 8.0 %attention.1 = bf16[512,2048]{1,0:T(8,128)(2,1)} custom-call(bf16[512,512]{1,0:T(8,128)(2,1)} %bitcast.34, bf16[512,512]{1,0:T(8,128)(2,1)} %bitcast.24, bf16[512,512]{1,0:T(8,128)(2,1)} %bitcast.26, bf16[512,128]{1,0:T(8,128)(2,1)} %bitcast.32, f32[1,512]{1,0:T(1,128)} %bitcast.38, bf16[512,2048]{1,0:T(8,128)(2,1)} %w_ref.1), custom_call_target="tpu_custom_call" | custom-call | tf_op jit(solution)/shard_map/attention/pallas_call | solution.py:216
  63.7 0.0 copy-start.2
  63.7 5.0 %all-to-all-start.2 = ((bf16[4,128,2048]{2,1,0:T(8,128)(2,1)}), bf16[4,128,2048]{2,1,0:T(8,128)(2,1)S(1)}, u32[]{:S(2)}, u32[]{:S(2)}) async-start(bf16[4,128,2048]{2,1,0:T(8,128)(2,1)} %bitcast.19), calls=%async_computation.2 | async-start | bytes 4194304 | tf_op jit(solution)/shard_map/all_to_all | solution.py:231
  68.7 0.0 copy-done.2
  68.7 0.7 copy.13
  69.4 1.9 slots.1
  71.3 19.0 %all-to-all-done.2.recv_ref = bf16[4,128,2048]{2,1,0:T(8,128)(2,1)S(1)} async-done(((bf16[4,128,2048]{2,1,0:T(8,128)(2,1)}), bf16[4,128,2048]{2,1,0:T(8,128)(2,1)S(1)}, u32[]{:S(2)}, u32[]{:S(2)}) %all-to-all-start.2) | async-done | bytes 2097184 | tf_op jit(solution)/shard_map/all_to_all | solution.py:231
  90.3 0.0 copy-start
  90.3 1.3 copy-done
  91.7 4.5 %dispatch.1 = (f32[128,2048]{1,0:T(8,128)}, bf16[1536,512]{1,0:T(8,128)(2,1)}) custom-call(bf16[4,128,2048]{2,1,0:T(8,128)(2,1)} %copy-done, bf16[128,2048]{1,0:T(8,128)(2,1)} %bitcast.31, f32[1,2048]{1,0:T(1,128)} %bitcast.37, s32[8,128]{1,0:T(8,128)} %get-tuple-element.9.rows_ref), custom_call_target="tpu_custom_call" | custom-call | tf_op jit(solution)/shard_map/dispatch/pallas_call | solution.py:233
  96.2 49.8 %all_to_all.50 = bf16[64,24,512]{2,1,0:T(8,128)(2,1)} all-to-all(bf16[64,24,512]{2,1,0:T(8,128)(2,1)} %bitcast.27), channel_id=1, replica_groups=mesh['seq'=16,'exp'=16,'head'=4] {'exp','head'}, dimensions={0} | all-to-all | bytes 3145728 | tf_op jit(solution)/shard_map/all_to_all | solution.py:243
  146.0 9.5 %experts.1 = bf16[1536,512]{1,0:T(8,128)(2,1)} custom-call(bf16[1536,512]{1,0:T(8,128)(2,1)} %bitcast.22, bf16[2048,384]{1,0:T(8,128)(2,1)} %bitcast.28, bf16[2048,384]{1,0:T(8,128)(2,1)} %bitcast.29, bf16[384,2048]{1,0:T(8,128)(2,1)} %bitcast.30), custom_call_target="tpu_custom_call" | custom-call | tf_op jit(solution)/shard_map/experts/pallas_call | solution.py:244
  155.5 0.0 copy-start.3
  155.5 5.6 %all-to-all-start.4 = ((bf16[64,24,512]{2,1,0:T(8,128)(2,1)}), bf16[64,24,512]{2,1,0:T(8,128)(2,1)S(1)}, u32[]{:S(2)}, u32[]{:S(2)}) async-start(bf16[64,24,512]{2,1,0:T(8,128)(2,1)} %bitcast.21), calls=%async_computation.4 | async-start | bytes 3145728 | tf_op jit(solution)/shard_map/all_to_all | solution.py:252
  161.1 0.0 copy-done.3
  161.1 0.7 copy.14
  161.8 39.3 %all-to-all-done.4 = bf16[64,24,512]{2,1,0:T(8,128)(2,1)S(1)} async-done(((bf16[64,24,512]{2,1,0:T(8,128)(2,1)}), bf16[64,24,512]{2,1,0:T(8,128)(2,1)S(1)}, u32[]{:S(2)}, u32[]{:S(2)}) %all-to-all-start.4) | async-done | bytes 1572896 | tf_op jit(solution)/shard_map/all_to_all | solution.py:252
  201.1 0.0 copy-start.1
  201.1 1.1 copy-done.1
  202.2 3.7 %combine.1 = bf16[128,2048]{1,0:T(8,128)(2,1)} custom-call(bf16[1536,512]{1,0:T(8,128)(2,1)} %bitcast.20, f32[128,2048]{1,0:T(8,128)} %get-tuple-element.11.resid_ref, s32[128,128]{1,0:T(8,128)} %get-tuple-element.12.cols_ref, f32[128,2]{1,0:T(8,128)} %bitcast.35), custom_call_target="tpu_custom_call" | custom-call | tf_op jit(solution)/shard_map/combine/pallas_call | solution.py:253
Async XLA Ops:
  63.7 5.0 %copy-start.2 = (s32[1,128,2]{1,2,0:T(2,128)S(1)}, s32[1,128,2]{1,2,0:T(2,128)}, u32[]{:S(2)}) copy-start(s32[1,128,2]{1,2,0:T(2,128)} %param.18) | copy-start | bytes 3076
  63.7 26.6 %all-to-all-start.2 = ((bf16[4,128,2048]{2,1,0:T(8,128)(2,1)}), bf16[4,128,2048]{2,1,0:T(8,128)(2,1)S(1)}, u32[]{:S(2)}, u32[]{:S(2)}) async-start(bf16[4,128,2048]{2,1,0:T(8,128)(2,1)} %bitcast.19), calls=%async_computation.2 | async-start | bytes 4194304 | tf_op jit(solution)/shard_map/all_to_all | solution.py:231
  90.3 1.3 copy-start
  155.5 5.6 %copy-start.3 = (f32[1,128,2]{1,2,0:T(2,128)S(1)}, f32[1,128,2]{1,2,0:T(2,128)}, u32[]{:S(2)}) copy-start(f32[1,128,2]{1,2,0:T(2,128)} %param.19) | copy-start | bytes 3076
  155.5 45.6 %all-to-all-start.4 = ((bf16[64,24,512]{2,1,0:T(8,128)(2,1)}), bf16[64,24,512]{2,1,0:T(8,128)(2,1)S(1)}, u32[]{:S(2)}, u32[]{:S(2)}) async-start(bf16[64,24,512]{2,1,0:T(8,128)(2,1)} %bitcast.21), calls=%async_computation.4 | async-start | bytes 3145728 | tf_op jit(solution)/shard_map/all_to_all | solution.py:252
  201.1 1.1 copy-start.1

commit v2 on v1

v2 whole, which is shorter than its diff:
```python
import functools
import math

import jax
import jax.numpy as jnp
from jax import lax
from jax.experimental import pallas as pl
from jax.experimental.pallas import tpu as pltpu
from jax.sharding import PartitionSpec as P

HEAD_DIM = 128
TOPK = 2
CAP = 6
QUARTERS = 4
GROUP = 8
EPSILON = 1e-06

BF16 = jnp.bfloat16
F32 = jnp.float32
I32 = jnp.int32


def vmem():
    return pl.BlockSpec(memory_space=pltpu.VMEM)


def call(kernel, args, out_shape, *, name, flops=10**6, limit=24, in_specs=None, **kwargs):
    outs = out_shape if isinstance(out_shape, tuple) else (out_shape,)
    if "out_specs" not in kwargs:
        kwargs["out_specs"] = tuple(vmem() for _ in outs) if isinstance(out_shape, tuple) else vmem()
    moved = sum(math.prod(a.shape) * jnp.dtype(a.dtype).itemsize for a in (*args, *outs))
    return pl.pallas_call(
        kernel,
        out_shape=out_shape,
        in_specs=in_specs or [vmem()] * len(args),
        cost_estimate=pl.CostEstimate(flops=flops, bytes_accessed=moved, transcendentals=0),
        compiler_params=pltpu.CompilerParams(vmem_limit_bytes=limit * 2**20),
        name=name,
        **kwargs,
    )(*args)


def dot(a, b, dims=((1,), (0,))):
    return lax.dot_general(a, b, (dims, ((), ())), preferred_element_type=F32)


def states_kernel(keys_ref, values_ref, out_ref):
    heads = keys_ref.shape[1] // HEAD_DIM
    for h in range(heads):
        cols = slice(h * HEAD_DIM, (h + 1) * HEAD_DIM)
        state = dot(keys_ref[:, cols], values_ref[:, cols], ((0,), (0,)))
        out_ref[cols, :] = state.astype(out_ref.dtype)


def scan_kernel(in_ref, out_ref):
    blocks = in_ref.shape[0]
    total = jnp.zeros(in_ref.shape[1:], F32)
    for b in range(blocks):
        out_ref[b] = total.astype(out_ref.dtype)
        total = total + in_ref[b].astype(F32)


def slots_kernel(routes_ref, cols_ref, pick_ref, *, experts):
    rows = routes_ref.shape[0]
    first, second = routes_ref[:, 0:1], routes_ref[:, 1:2]
    ids = lax.broadcasted_iota(I32, (rows, experts), 1)
    hit0 = (first == ids).astype(F32)
    hit1 = (second == ids).astype(F32)
    above = lax.broadcasted_iota(I32, (rows, rows), 0) > lax.broadcasted_iota(I32, (rows, rows), 1)
    before = dot(above.astype(F32).astype(BF16), (hit0 + hit1).astype(BF16))
    pos0 = jnp.sum(before * hit0, axis=1, keepdims=True)
    pos1 = jnp.sum(before * hit1, axis=1, keepdims=True)
    slot0 = first.astype(F32) * CAP + pos0
    slot1 = second.astype(F32) * CAP + pos1
    lane = lax.broadcasted_iota(I32, (rows, 128), 1)
    both = jnp.where(lane == 0, slot0, jnp.where(lane == 1, slot1, 0.0))
    cols_ref[...] = both.astype(I32)
    slots = both.T.astype(I32)
    key0 = jnp.concatenate([slots[0:1] * QUARTERS + q for q in range(QUARTERS)], axis=1)
    key1 = jnp.concatenate([slots[1:2] * QUARTERS + q for q in range(QUARTERS)], axis=1)
    total = pick_ref.shape[0]
    chunk = total // 4
    for b in range(4):
        keys = row_keys(chunk, b * chunk)
        pick = ((keys == key0) | (keys == key1)).astype(F32)
        pick_ref[b * chunk : (b + 1) * chunk, :] = pick.astype(BF16)


def inner_kernel(query_ref, keys_ref, values_ref, after_ref, out_ref):
    length = keys_ref.shape[0]
    heads = query_ref.shape[1] // HEAD_DIM
    rows = length // 4
    for i in range(4):
        seen = (i + 1) * rows
        row_ids = lax.broadcasted_iota(I32, (rows, seen), 0) + i * rows
        causal = row_ids >= lax.broadcasted_iota(I32, (rows, seen), 1)
        for h in range(heads):
            cols = slice(h * HEAD_DIM, (h + 1) * HEAD_DIM)
            q = query_ref[i * rows : (i + 1) * rows, cols]
            scores = dot(q, keys_ref[0:seen, cols], ((1,), (1,)))
            scores = jnp.where(causal, scores, 0.0).astype(BF16)
            out_ref[i * rows : (i + 1) * rows, cols] = dot(scores, values_ref[0:seen, cols])


def project_kernel(inner_ref, query_ref, prefix_ref, gain_ref, w_ref, out_ref, normed_ref, part_ref, sems):
    heads = query_ref.shape[1] // HEAD_DIM
    for h in range(heads):
        cols = slice(h * HEAD_DIM, (h + 1) * HEAD_DIM)
        out = inner_ref[:, cols] + dot(query_ref[:, cols], prefix_ref[cols, :])
        scale = lax.rsqrt(jnp.mean(out * out, axis=-1, keepdims=True) + EPSILON)
        normed_ref[:, cols] = (out * scale * gain_ref[:, cols]).astype(BF16)
    steps, _, _, part = part_ref.shape
    copies = []
    for j in range(steps):
        cols = slice(j * part, (j + 1) * part)
        part_ref[j] = dot(normed_ref[...], w_ref[:, cols]).astype(BF16).reshape(part_ref.shape[1:])
        copies.append(pltpu.make_async_copy(part_ref.at[j], out_ref.at[:, :, cols], sems.at[j]))
        copies[-1].start()
    for copy in copies:
        copy.wait()


def row_keys(count, base):
    piece = QUARTERS * CAP
    r = lax.broadcasted_iota(I32, (count, 1), 0).astype(F32) + base
    e = jnp.floor((r + 0.5) * (1.0 / piece))
    rem = r - e * piece
    q = jnp.floor((rem + 0.5) * (1.0 / CAP))
    c = rem - q * CAP
    return (QUARTERS * (e * CAP + c) + q).astype(I32)


def dispatch_kernel(recv_ref, tokens_ref, gain_ref, pick_ref, resid_ref, out_ref):
    peers = recv_ref.shape[0]
    width = tokens_ref.shape[1]
    attn = recv_ref[0].astype(F32)
    for p in range(1, peers):
        attn = attn + recv_ref[p].astype(F32)
    resid = tokens_ref[...].astype(F32) + attn
    resid_ref[...] = resid
    scale = lax.rsqrt(jnp.mean(resid * resid, axis=-1, keepdims=True) + EPSILON)
    moe_in = (resid * scale * gain_ref[...]).astype(BF16)
    part = width // QUARTERS
    stacked = jnp.concatenate([moe_in[:, q * part : (q + 1) * part] for q in range(QUARTERS)], axis=0)
    out_ref[...] = dot(pick_ref[...], stacked).astype(BF16)


def regroup_matrix(to_pieces):
    n = GROUP * QUARTERS * CAP
    i = lax.broadcasted_iota(I32, (n, 1), 0).astype(F32)
    q = jnp.floor((i + 0.5) * (1.0 / (GROUP * CAP)))
    rem = i - q * (GROUP * CAP)
    p = jnp.floor((rem + 0.5) * (1.0 / CAP))
    c = rem - p * CAP
    source = (p * (QUARTERS * CAP) + q * CAP + c).astype(I32)
    j = lax.broadcasted_iota(I32, (n, n), 1)
    matrix = (source == j).astype(F32)
    if to_pieces:
        matrix = matrix.T
    return matrix.astype(BF16)


def expert_kernel(recv_ref, gate_ref, up_ref, down_ref, out_ref, x_ref, y_ref, z_ref, sems):
    rows, part = recv_ref.shape
    n = GROUP * QUARTERS * CAP
    m = n // QUARTERS
    gather = regroup_matrix(False)
    for g in range(rows // n):
        block = dot(gather, recv_ref[g * n : (g + 1) * n, :]).astype(BF16)
        for q in range(QUARTERS):
            x_ref[g * m : (g + 1) * m, q * part : (q + 1) * part] = block[q * m : (q + 1) * m, :]
    x = x_ref[...]
    gate = dot(x, gate_ref[...])
    up = dot(x, up_ref[...])
    hidden = (gate / (1.0 + jnp.exp(-gate)) * up).astype(BF16)
    for q in range(QUARTERS):
        made = dot(hidden, down_ref[:, q * part : (q + 1) * part]).astype(BF16)
        for g in range(rows // n):
            y_ref[g * n + q * m : g * n + (q + 1) * m, :] = made[g * m : (g + 1) * m, :]
    scatter = regroup_matrix(True)
    copies = []
    for g in range(rows // n):
        part_rows = slice(g * n, (g + 1) * n)
        z_ref[part_rows, :] = dot(scatter, y_ref[part_rows, :]).astype(BF16)
        copies.append(pltpu.make_async_copy(z_ref.at[part_rows], out_ref.at[part_rows], sems.at[g]))
        copies[-1].start()
    for copy in copies:
        copy.wait()


def combine_kernel(back_ref, resid_ref, cols_ref, gates_ref, out_ref, y_ref):
    rows, part = back_ref.shape
    tok_rows = resid_ref.shape[0]
    n = GROUP * QUARTERS * CAP
    m = n // QUARTERS
    gather = regroup_matrix(False)
    for g in range(rows // n):
        block = dot(gather, back_ref[g * n : (g + 1) * n, :]).astype(BF16)
        for q in range(QUARTERS):
            y_ref[g * m : (g + 1) * m, q * part : (q + 1) * part] = block[q * m : (q + 1) * m, :]
    y = y_ref[...]
    slot_total = y.shape[0]
    ids = lax.broadcasted_iota(I32, (tok_rows, slot_total), 1)
    total = resid_ref[...]
    moe = jnp.zeros_like(total)
    for pick in range(TOPK):
        chosen = (cols_ref[:, pick : pick + 1] == ids).astype(F32).astype(BF16)
        moe = moe + gates_ref[:, pick : pick + 1] * dot(chosen, y)
    out_ref[...] = (total + moe).astype(out_ref.dtype)


def on_device(
    query, keys, values, attn_gain, w_out, tokens, routes, gates, moe_gain, w_gate, w_up, w_down
):
    query, keys, values = query[0], keys[0], values[0]
    tokens, routes, gates = tokens[0], routes[0], gates[0]
    w_gate, w_up, w_down = w_gate[0], w_up[0], w_down[0]
    length, feat = query.shape
    tok_rows, width = tokens.shape
    n_seq, n_exp, n_head = (lax.axis_size(a) for a in ("seq", "exp", "head"))
    experts = n_exp * n_head
    part = width // QUARTERS
    piece = QUARTERS * CAP

    states = call(
        states_kernel,
        (keys, values),
        jax.ShapeDtypeStruct((feat, HEAD_DIM), BF16),
        name="states",
        flops=2 * length * feat * HEAD_DIM,
    )
    spread = lax.all_to_all(states, "seq", split_axis=0, concat_axis=0, tiled=True)
    inner = call(
        inner_kernel,
        (query, keys, values, states),
        jax.ShapeDtypeStruct((length, feat), F32),
        in_specs=[vmem()] * 3 + [pl.BlockSpec(memory_space=pl.ANY)],
        name="inner",
        flops=4 * length * length * feat,
    )
    slot_cols, pick = call(
        functools.partial(slots_kernel, experts=experts),
        (routes,),
        (
            jax.ShapeDtypeStruct((tok_rows, 128), I32),
            jax.ShapeDtypeStruct((experts * piece, QUARTERS * tok_rows), BF16),
        ),
        name="slots",
        flops=10**8,
    )
    scanned = call(
        scan_kernel,
        (spread.reshape(n_seq, feat // n_seq, HEAD_DIM),),
        jax.ShapeDtypeStruct((n_seq, feat // n_seq, HEAD_DIM), BF16),
        name="scan",
    )
    prefix = lax.all_to_all(
        scanned.reshape(feat, HEAD_DIM), "seq", split_axis=0, concat_axis=0, tiled=True
    )
    partial_out = call(
        project_kernel,
        (inner, query, prefix, attn_gain.reshape(1, feat), w_out),
        pltpu.HBM((n_head, tok_rows, width), BF16),
        out_specs=pl.BlockSpec(memory_space=pltpu.HBM),
        scratch_shapes=[
            pltpu.VMEM((length, feat), BF16),
            pltpu.VMEM((QUARTERS, n_head, tok_rows, part), BF16),
            pltpu.SemaphoreType.DMA((QUARTERS,)),
        ],
        name="project",
        flops=2 * length * feat * width,
    )
    summed = lax.all_to_all(partial_out, "head", split_axis=0, concat_axis=0, tiled=False)

    resid, sent = call(
        dispatch_kernel,
        (summed.reshape(n_head, tok_rows, width), tokens, moe_gain.reshape(1, width), pick),
        (
            jax.ShapeDtypeStruct((tok_rows, width), F32),
            jax.ShapeDtypeStruct((experts * piece, part), BF16),
        ),
        name="dispatch",
        flops=2 * experts * piece * QUARTERS * tok_rows * part,
    )
    received = lax.all_to_all(sent, ("exp", "head"), split_axis=0, concat_axis=0, tiled=True)
    made = call(
        expert_kernel,
        (received, w_gate, w_up, w_down),
        jax.ShapeDtypeStruct((experts * piece, part), BF16),
        scratch_shapes=[
            pltpu.VMEM((experts * CAP, width), BF16),
            pltpu.VMEM((experts * piece, part), BF16),
            pltpu.VMEM((experts * piece, part), BF16),
            pltpu.SemaphoreType.DMA((experts // GROUP,)),
        ],
        out_specs=pl.BlockSpec(memory_space=pltpu.HBM),
        name="experts",
        flops=6 * experts * CAP * width * w_gate.shape[1],
    )
    returned = lax.all_to_all(made, ("exp", "head"), split_axis=0, concat_axis=0, tiled=True)
    mixed = call(
        combine_kernel,
        (returned, resid, slot_cols, gates),
        jax.ShapeDtypeStruct((tok_rows, width), BF16),
        scratch_shapes=[pltpu.VMEM((experts * CAP, width), BF16)],
        name="combine",
        flops=10**9,
    )
    return mixed[None]


def solution(mesh):
    in_specs = (
        P("exp", "seq", "head"),
        P("exp", "seq", "head"),
        P("exp", "seq", "head"),
        P("head"),
        P("head", None),
        P("exp", ("seq", "head"), None),
        P("exp", ("seq", "head"), None),
        P("exp", ("seq", "head"), None),
        P(),
        P(("exp", "head"), None, None),
        P(("exp", "head"), None, None),
        P(("exp", "head"), None, None),
    )
    out_specs = P("exp", ("seq", "head"), None)
    return jax.shard_map(
        on_device, mesh=mesh, in_specs=in_specs, out_specs=out_specs, check_vma=False
    )
```

time: 207 us -> 191 us (0.923)
  blocking collectives: 102 us -> 83.2 us
  Pallas kernels: 31.4 us -> 15 us
  waiting for transfers between devices: 58.3 us -> 67.9 us
  local copies, waits for them, and re-layouts: 3.96 us -> 10 us
  starting transfers between devices: 10.5 us -> 14.4 us
    all_to_all x1 -> x0, blocking collectives: 18.2 us -> none  [on_device(): lax.all_to_all(scanned.reshape(feat, HEAD_DIM), 'seq', split_axis=0, conc...]
    pallas_call x7 -> x8, Pallas kernels: 31.4 us -> 15 us  [call(): pl.pallas_call(kernel, out_shape=out_shape, in_specs=in_specs or [vmem()]...]
    all_to_all x1 -> x2, waiting for transfers between devices: 19 us -> 28 us  [the longest x1 19.3 us: on_device(): lax.all_to_all(partial_out, 'head', split_axis=0, concat_axis=0, tiled=Fa...]
    unnamed x10 -> x40, local copies, waits for them, and re-layouts: 3.96 us -> 10 us
    all_to_all x1 -> x2, starting transfers between devices: 4.98 us -> 8.85 us  [the longest x1 4.97 us: on_device(): lax.all_to_all(partial_out, 'head', split_axis=0, concat_axis=0, tiled=Fa...]
  transfers between devices with their start and end apart: 2 -> 3, of which waited for: 2 -> 3; matrix products, arithmetic and copies ran while one was open for 1% -> 0% of each run, Pallas kernels for 1% -> 2%
where the time goes in v2:
time: 191 us
  blocking collectives  83.2 us (44%)
  waiting for transfers between devices  67.9 us (36%)
  Pallas kernels  15 us (8%)
  starting transfers between devices  14.4 us (8%)
  local copies, waits for them, and re-layouts  10 us (5%)
    all_to_all x1, blocking collectives, on_device(): lax.all_to_all(sent, ('exp', 'head'), split_axis=0, concat_axis=0, tiled=...  49.8 us
    all_to_all x1, waiting for transfers between devices, on_device(): lax.all_to_all(made, ('exp', 'head'), split_axis=0, concat_axis=0, tiled=...  39.9 us
    all_to_all x1, blocking collectives, on_device(): lax.all_to_all(states, 'seq', split_axis=0, concat_axis=0, tiled=True)  33.5 us
    all_to_all x1, waiting for transfers between devices, on_device(): lax.all_to_all(partial_out, 'head', split_axis=0, concat_axis=0, tiled=Fa...  19.3 us
    pallas_call x8, Pallas kernels, call(): pl.pallas_call(kernel, out_shape=out_shape, in_specs=in_specs or [vmem()]...  15 us
    unnamed x40, local copies, waits for them, and re-layouts  10 us
    all_to_all x1, waiting for transfers between devices, on_device(): lax.all_to_all(scanned.reshape(feat, HEAD_DIM), 'seq', split_axis=0, conc...  8.73 us
    all_to_all x1, starting transfers between devices, on_device(): lax.all_to_all(made, ('exp', 'head'), split_axis=0, concat_axis=0, tiled=...  5.56 us
  transfers between devices with their start and end apart: 3, of which 3 were waited for; matrix products, arithmetic and copies ran while one was open for 0% of the time, Pallas kernels for 2%

profile of v2, /device:TPU:2, one launch (start us, length us, event | category | flops | bytes accessed | tf_op | source)
XLA Modules:
  0.0 190.7 jit_solution(8746858455949387653)
XLA Ops:
  0.0 0.0 copy-start.1
  0.0 1.0 copy-done.1
  1.0 0.0 copy-start.3
  1.0 1.0 copy-done.3
  2.1 0.3 states.1.after_ref
  2.4 33.5 %all_to_all.44.in_ref = bf16[16,32,128]{2,1,0:T(8,128)(2,1)S(1)} all-to-all(bf16[16,32,128]{2,1,0:T(8,128)(2,1)S(1)} %bitcast.30), channel_id=1, replica_groups=mesh['seq'=16,'exp'=16,'head'=4] {'seq'}, dimensions={0} | all-to-all | bytes 262144 | tf_op jit(solution)/shard_map/all_to_all | solution.py:232
  35.9 0.7 scan.1
  36.6 0.0 copy-start
  36.6 3.9 %all-to-all-start.1 = ((bf16[16,32,128]{2,1,0:T(8,128)(2,1)}), bf16[16,32,128]{2,1,0:T(8,128)(2,1)S(1)}, u32[]{:S(2)}, u32[]{:S(2)}) async-start(bf16[16,32,128]{2,1,0:T(8,128)(2,1)} %scan.1), calls=%async_computation.1 | async-start | bytes 262144 | tf_op jit(solution)/shard_map/all_to_all | solution.py:257
  40.5 0.0 copy-start.2
  40.5 1.0 copy-done.2
  41.5 1.0 copy-done.4
  42.5 1.0 copy-done.5
  43.6 2.4 %inner.1.inner_ref = f32[512,512]{1,0:T(8,128)S(1)} custom-call(bf16[512,512]{1,0:T(8,128)(2,1)S(1)} %bitcast.23, bf16[512,512]{1,0:T(8,128)(2,1)S(1)} %bitcast.20, bf16[512,512]{1,0:T(8,128)(2,1)S(1)} %bitcast.22, bf16[512,128]{1,0:T(8,128)(2,1)S(1)} %states.1.after_ref), custom_call_target="tpu_custom_call" | custom-call | flops 536870912 | bytes 2752512 | tf_op jit(solution)/shard_map/inner/pallas_call | solution.py:32
  46.0 8.7 %all-to-all-done.1 = bf16[16,32,128]{2,1,0:T(8,128)(2,1)S(1)} async-done(((bf16[16,32,128]{2,1,0:T(8,128)(2,1)}), bf16[16,32,128]{2,1,0:T(8,128)(2,1)S(1)}, u32[]{:S(2)}, u32[]{:S(2)}) %all-to-all-start.1) | async-done | bytes 131104 | tf_op jit(solution)/shard_map/all_to_all | solution.py:257
  54.7 0.0 copy-done.14
  54.7 0.0 copy-done
  54.7 1.0 copy-done.6
  55.8 2.5 %project.1 = bf16[4,128,2048]{2,1,0:T(8,128)(2,1)} custom-call(f32[512,512]{1,0:T(8,128)S(1)} %inner.1.inner_ref, bf16[512,512]{1,0:T(8,128)(2,1)S(1)} %bitcast.24, bf16[512,128]{1,0:T(8,128)(2,1)S(1)} %bitcast.31, f32[1,512]{1,0:T(1,128)S(1)} %bitcast.36, bf16[512,2048]{1,0:T(8,128)(2,1)S(1)} %copy-done), custom_call_target="tpu_custom_call" | custom-call | flops 1073741824 | bytes 5900288 | tf_op jit(solution)/shard_map/project/pallas_call | solution.py:32
  58.2 0.0 copy-start.17
  58.3 0.0 copy-start.12
  58.3 0.0 copy-start.13
  58.3 5.0 %all-to-all-start.2 = ((bf16[4,128,2048]{2,1,0:T(8,128)(2,1)}), bf16[4,128,2048]{2,1,0:T(8,128)(2,1)S(1)}, u32[]{:S(2)}, u32[]{:S(2)}) async-start(bf16[4,128,2048]{2,1,0:T(8,128)(2,1)} %project.1), calls=%async_computation.2 | async-start | bytes 4194304 | tf_op jit(solution)/shard_map/all_to_all | solution.py:273
  63.3 0.0 copy-done.17
  63.3 0.1 copy.13
  63.4 1.2 slots.1
  64.6 0.0 copy-start.7
  64.6 1.1 copy-done.7
  65.7 19.3 %all-to-all-done.2.recv_ref = bf16[4,128,2048]{2,1,0:T(8,128)(2,1)S(1)} async-done(((bf16[4,128,2048]{2,1,0:T(8,128)(2,1)}), bf16[4,128,2048]{2,1,0:T(8,128)(2,1)S(1)}, u32[]{:S(2)}, u32[]{:S(2)}) %all-to-all-start.2) | async-done | bytes 2097184 | tf_op jit(solution)/shard_map/all_to_all | solution.py:273
  85.0 0.0 copy-done.12
  85.0 0.0 copy-done.13
  85.0 1.4 copy-done.8
  86.4 1.4 dispatch.1
  87.9 0.0 copy-start.15
  87.9 1.0 copy-done.15
  88.9 49.8 %all_to_all.45 = bf16[64,24,512]{2,1,0:T(8,128)(2,1)S(1)} all-to-all(bf16[64,24,512]{2,1,0:T(8,128)(2,1)S(1)} %bitcast.26), channel_id=1, replica_groups=mesh['seq'=16,'exp'=16,'head'=4] {'exp','head'}, dimensions={0} | all-to-all | bytes 3145728 | tf_op jit(solution)/shard_map/all_to_all | solution.py:285
  138.7 0.0 copy-done.11
  138.7 0.0 copy-done.9
  138.7 0.0 copy-done.10
  138.7 4.4 %experts.1 = bf16[1536,512]{1,0:T(8,128)(2,1)} custom-call(bf16[1536,512]{1,0:T(8,128)(2,1)S(1)} %bitcast.18, bf16[2048,384]{1,0:T(8,128)(2,1)S(1)} %bitcast.27, bf16[2048,384]{1,0:T(8,128)(2,1)S(1)} %bitcast.28, bf16[384,2048]{1,0:T(8,128)(2,1)S(1)} %bitcast.29), custom_call_target="tpu_custom_call" | custom-call | flops 1811939328 | bytes 7864320 | tf_op jit(solution)/shard_map/experts/pallas_call | solution.py:32
  143.1 0.0 copy-start.18
  143.1 0.0 copy-start.16
  143.1 5.6 %all-to-all-start.4 = ((bf16[64,24,512]{2,1,0:T(8,128)(2,1)}), bf16[64,24,512]{2,1,0:T(8,128)(2,1)S(1)}, u32[]{:S(2)}, u32[]{:S(2)}) async-start(bf16[64,24,512]{2,1,0:T(8,128)(2,1)} %bitcast.14), calls=%async_computation.4 | async-start | bytes 3145728 | tf_op jit(solution)/shard_map/all_to_all | solution.py:300
  148.7 0.0 copy-done.18
  148.7 0.1 copy.14
  148.8 39.9 %all-to-all-done.4 = bf16[64,24,512]{2,1,0:T(8,128)(2,1)S(1)} async-done(((bf16[64,24,512]{2,1,0:T(8,128)(2,1)}), bf16[64,24,512]{2,1,0:T(8,128)(2,1)S(1)}, u32[]{:S(2)}, u32[]{:S(2)}) %all-to-all-start.4) | async-done | bytes 1572896 | tf_op jit(solution)/shard_map/all_to_all | solution.py:300
  188.7 0.0 copy-done.16
  188.7 2.0 %combine.1 = bf16[128,2048]{1,0:T(8,128)(2,1)} custom-call(bf16[1536,512]{1,0:T(8,128)(2,1)S(1)} %bitcast.25, f32[128,2048]{1,0:T(8,128)S(1)} %copy-done.16, s32[128,128]{1,0:T(8,128)S(1)} %get-tuple-element.12.cols_ref, f32[128,2]{1,0:T(8,128)S(1)} %bitcast.33), custom_call_target="tpu_custom_call" | custom-call | flops 1000000000 | bytes 3212288 | tf_op jit(solution)/shard_map/combine/pallas_call | solution.py:32
  (8 shorter events, 0.0 us)
Async XLA Ops:
  0.0 1.0 copy-start.1
  1.0 1.0 copy-start.3
  35.9 18.8 %copy-start.14 = (f32[512]{0:T(512)S(1)}, f32[512]{0:T(512)}, u32[]{:S(2)}) copy-start(f32[512]{0:T(512)} %param.15) | copy-start | bytes 6148
  36.6 18.1 %copy-start = (bf16[512,2048]{1,0:T(8,128)(2,1)S(1)}, bf16[512,2048]{1,0:T(8,128)(2,1)}, u32[]{:S(2)}) copy-start(bf16[512,2048]{1,0:T(8,128)(2,1)} %w_ref.1) | copy-start | bytes 6291460
  36.6 18.1 %all-to-all-start.1 = ((bf16[16,32,128]{2,1,0:T(8,128)(2,1)}), bf16[16,32,128]{2,1,0:T(8,128)(2,1)S(1)}, u32[]{:S(2)}, u32[]{:S(2)}) async-start(bf16[16,32,128]{2,1,0:T(8,128)(2,1)} %scan.1), calls=%async_computation.1 | async-start | bytes 262144 | tf_op jit(solution)/shard_map/all_to_all | solution.py:257
  40.5 1.0 copy-start.2
  41.5 1.0 copy-start.4
  42.5 1.0 copy-start.5
  54.7 1.0 copy-start.6
  58.2 5.0 %copy-start.17 = (s32[1,128,2]{1,2,0:T(2,128)S(1)}, s32[1,128,2]{1,2,0:T(2,128)}, u32[]{:S(2)}) copy-start(s32[1,128,2]{1,2,0:T(2,128)} %param.18) | copy-start | bytes 3076
  58.3 26.8 %copy-start.12 = (bf16[1,128,2048]{2,1,0:T(8,128)(2,1)S(1)}, bf16[1,128,2048]{2,1,0:T(8,128)(2,1)}, u32[]{:S(2)}) copy-start(bf16[1,128,2048]{2,1,0:T(8,128)(2,1)} %param.17) | copy-start | bytes 1572868
  58.3 26.8 %copy-start.13 = (f32[2048]{0:T(1024)S(1)}, f32[2048]{0:T(1024)}, u32[]{:S(2)}) copy-start(f32[2048]{0:T(1024)} %param.20) | copy-start | bytes 24580
  58.3 26.7 %all-to-all-start.2 = ((bf16[4,128,2048]{2,1,0:T(8,128)(2,1)}), bf16[4,128,2048]{2,1,0:T(8,128)(2,1)S(1)}, u32[]{:S(2)}, u32[]{:S(2)}) async-start(bf16[4,128,2048]{2,1,0:T(8,128)(2,1)} %project.1), calls=%async_computation.2 | async-start | bytes 4194304 | tf_op jit(solution)/shard_map/all_to_all | solution.py:273
  64.6 1.1 copy-start.7
  85.0 1.4 copy-start.8
  86.4 52.2 %copy-start.11 = (bf16[1,384,2048]{2,1,0:T(8,128)(2,1)S(1)}, bf16[1,384,2048]{2,1,0:T(8,128)(2,1)}, u32[]{:S(2)}) copy-start(bf16[1,384,2048]{2,1,0:T(8,128)(2,1)} %param.23) | copy-start | bytes 4718596
  87.9 1.0 copy-start.15
  88.9 49.8 %copy-start.9 = (bf16[1,2048,384]{2,1,0:T(8,128)(2,1)S(1)}, bf16[1,2048,384]{2,1,0:T(8,128)(2,1)}, u32[]{:S(2)}) copy-start(bf16[1,2048,384]{2,1,0:T(8,128)(2,1)} %param.21) | copy-start | bytes 4718596
  88.9 49.8 %copy-start.10 = (bf16[1,2048,384]{2,1,0:T(8,128)(2,1)S(1)}, bf16[1,2048,384]{2,1,0:T(8,128)(2,1)}, u32[]{:S(2)}) copy-start(bf16[1,2048,384]{2,1,0:T(8,128)(2,1)} %param.22) | copy-start | bytes 4718596
  143.1 5.6 %copy-start.18 = (f32[1,128,2]{1,2,0:T(2,128)S(1)}, f32[1,128,2]{1,2,0:T(2,128)}, u32[]{:S(2)}) copy-start(f32[1,128,2]{1,2,0:T(2,128)} %param.19) | copy-start | bytes 3076
  143.1 45.6 %copy-start.16 = (f32[128,2048]{1,0:T(8,128)S(1)}, f32[128,2048]{1,0:T(8,128)}, u32[]{:S(2)}) copy-start(f32[128,2048]{1,0:T(8,128)} %copy-done.15) | copy-start | bytes 3145732
  143.1 45.6 %all-to-all-start.4 = ((bf16[64,24,512]{2,1,0:T(8,128)(2,1)}), bf16[64,24,512]{2,1,0:T(8,128)(2,1)S(1)}, u32[]{:S(2)}, u32[]{:S(2)}) async-start(bf16[64,24,512]{2,1,0:T(8,128)(2,1)} %bitcast.14), calls=%async_computation.4 | async-start | bytes 3145728 | tf_op jit(solution)/shard_map/all_to_all | solution.py:300
